TPU v7x, 32 devices: a whole 2x2x4 slice. The times are simulated.
32 devices in a mesh: dp: 2 (over core), row: 4 (over y, x), col: 4 (over z).
Axes of the slice: x: 2, y: 2, z: 4, core: 2. Of those that a mesh axis runs over, the one named last changes fastest.
Arguments:
- tokens: bfloat16 [768, 8192], P('row', ('dp', 'col')), may hold values from -6 to 6
- prefix: int32 [8], P(('dp', 'row')), may hold values from 102 to 512, as said below
- ln1_gain: float32 [768], replicated, may hold values from 0.5 to 1.5
- ln1_bias: float32 [768], replicated, may hold values from -3 to 3
- w_qkv: bfloat16 [3, 768, 768], P(None, 'row', 'col'), may hold values from -0.21875 to 0.21875
- qv_bias: float32 [2, 768], replicated, may hold values from -3 to 3
- w_out: bfloat16 [768, 768], P('col', 'row'), may hold values from -0.875 to 0.875
- out_bias: float32 [768], replicated, may hold values from -3 to 3
- ln2_gain: float32 [768], replicated, may hold values from 0.5 to 1.5
- ln2_bias: float32 [768], replicated, may hold values from -3 to 3
- w_fc: bfloat16 [768, 3072], P('row', 'col'), may hold values from -0.21875 to 0.21875
- fc_bias: float32 [3072], replicated, may hold values from -3 to 3
- w_proj: bfloat16 [768, 3072], P('row', 'col'), may hold values from -0.109375 to 0.109375
- proj_bias: float32 [768], replicated, may hold values from -3 to 3
- cotangent: bfloat16 [768, 8192], P('row', ('dp', 'col')), may hold values from -6 to 6
Outputs:
- output: bfloat16 [768, 8192], P('row', ('dp', 'col'))
- input_grad: float32 [768, 8192], P('row', ('dp', 'col'))
- ln1_gain_grad: float32 [768], replicated
- ln1_bias_grad: float32 [768], replicated
- w_qkv_grad: float32 [3, 768, 768], P(None, 'row', 'col')
- qv_bias_grad: float32 [2, 768], replicated
- w_out_grad: float32 [768, 768], P('col', 'row')
- out_bias_grad: float32 [768], replicated
- ln2_gain_grad: float32 [768], replicated
- ln2_bias_grad: float32 [768], replicated
- w_fc_grad: float32 [768, 3072], P('row', 'col')
- fc_bias_grad: float32 [3072], replicated
- w_proj_grad: float32 [768, 3072], P('row', 'col')
- proj_bias_grad: float32 [768], replicated
Inputs may be any that keep to these rules, and one draw needn't show every extreme that they name: `prefix`: in every draw some sequence has exactly 102 and some other exactly 512.
All inputs are finite; a program needn't handle non-finite values.
Results may differ from a plain program's by a relative error of at most 0.012.
Values may be sent and summed in bfloat16 or wider, within the bound.
A program may use at most 256 MiB of HBM per device.

v0:
```python
import jax
import jax.numpy as jnp
from jax import lax
from jax.sharding import PartitionSpec as P

D = 768
FF = 3072
HEAD_DIM = 64
LEN = 1024
epsilon = 1e-05
masked_score = -1e30


def feature_totals(values):
    return lax.psum(values, "row")


def column_rows(values):
    return lax.all_gather(values, "col", axis=0, tiled=True)


def row_rows(values):
    return lax.all_gather(values, "row", axis=0, tiled=True)


def summed_over_row(term_fn, row_count):
    return lax.psum_scatter(
        term_fn(jnp.int32(0), row_count * lax.axis_size("row")),
        "row",
        scatter_dimension=0,
        tiled=True,
    )


def summed_over_col(term_fn, row_count):
    return lax.psum_scatter(
        term_fn(jnp.int32(0), row_count * lax.axis_size("col")),
        "col",
        scatter_dimension=0,
        tiled=True,
    )


def take_portion(complete, position, portion_size, along):
    return lax.dynamic_slice_in_dim(complete, position * portion_size, portion_size, along)


def place_portion(portion, position, full_size, along):
    zeroed_shape = portion.shape[:along] + (full_size,) + portion.shape[along + 1 :]
    zeroed = jnp.zeros(zeroed_shape, jnp.float32)
    return lax.dynamic_update_slice_in_dim(zeroed, portion, position * portion.shape[along], along)


def gelu_tanh(values):
    return jax.nn.gelu(values, approximate=True)


def norm_forward(values, norm_gain, norm_offset, totals_fn):
    plain_sum, square_sum = totals_fn((jnp.sum(values, axis=1), jnp.sum(values * values, axis=1)))
    center = (plain_sum / D)[:, None]
    inverse = lax.rsqrt(square_sum[:, None] / D - center * center + epsilon)
    unit_rows = (values - center) * inverse
    return (unit_rows * norm_gain + norm_offset, unit_rows, inverse)


def norm_backward(grad_rows, unit_rows, inverse, norm_gain, totals_fn):
    scaled = grad_rows * norm_gain
    plain_sum, cross_sum = totals_fn((jnp.sum(scaled, axis=1), jnp.sum(scaled * unit_rows, axis=1)))
    return inverse * (scaled - (plain_sum / D)[:, None] - unit_rows * (cross_sum / D)[:, None])


def split_heads(flat_rows):
    return flat_rows.reshape(LEN, flat_rows.shape[1] // HEAD_DIM, HEAD_DIM)


def scores_of(queries, keys_block, limit_value):
    raw_scores = jnp.einsum("qhe,khe->hqk", queries, keys_block, preferred_element_type=jnp.float32)
    raw_scores = raw_scores * HEAD_DIM ** (-0.5)
    places = jnp.arange(LEN, dtype=jnp.int32)
    visible = (places[None, :] <= places[:, None]) | (places[None, :] < limit_value)
    return jnp.where(visible[None], raw_scores, masked_score)


def attend_forward(packed):
    block_rows, limit_value = packed
    queries = split_heads(block_rows[:, 0])
    keys_block = split_heads(block_rows[:, 1])
    values_block = split_heads(block_rows[:, 2])
    scores = scores_of(queries, keys_block, limit_value)
    largest = jnp.max(scores, axis=-1, keepdims=True)
    weights = jnp.exp(scores - largest)
    row_totals = jnp.sum(weights, axis=-1, keepdims=True)
    probs = (weights / row_totals).astype(jnp.bfloat16)
    mixed = jnp.einsum("hqk,khe->qhe", probs, values_block, preferred_element_type=jnp.float32)
    return (mixed.reshape(LEN, -1).astype(jnp.bfloat16), (largest + jnp.log(row_totals))[..., 0])


def attend_backward(packed):
    block_rows, limit_value, log_total, out_grad = packed
    queries = split_heads(block_rows[:, 0])
    keys_block = split_heads(block_rows[:, 1])
    values_block = split_heads(block_rows[:, 2])
    scores = scores_of(queries, keys_block, limit_value)
    probs = jnp.exp(scores - log_total[..., None])
    probs_low = probs.astype(jnp.bfloat16)
    grad_heads = split_heads(out_grad)
    weight_grad = jnp.einsum(
        "qhe,khe->hqk", grad_heads, values_block, preferred_element_type=jnp.float32
    )
    row_inner = jnp.sum(probs * weight_grad, axis=-1, keepdims=True)
    score_grad = (probs * (weight_grad - row_inner)).astype(jnp.bfloat16)
    query_grad = jnp.einsum(
        "hqk,khe->qhe", score_grad, keys_block, preferred_element_type=jnp.float32
    )
    key_grad = jnp.einsum("hqk,qhe->khe", score_grad, queries, preferred_element_type=jnp.float32)
    value_grad = jnp.einsum(
        "hqk,qhe->khe", probs_low, grad_heads, preferred_element_type=jnp.float32
    )
    score_factor = HEAD_DIM ** (-0.5)
    stacked = jnp.stack(
        [
            (query_grad * score_factor).reshape(LEN, -1),
            (key_grad * score_factor).reshape(LEN, -1),
            value_grad.reshape(LEN, -1),
        ],
        axis=1,
    )
    return stacked.astype(jnp.bfloat16)


def on_device(
    tokens,
    prefix,
    ln1_gain,
    ln1_bias,
    w_qkv,
    qv_bias,
    w_out,
    out_bias,
    ln2_gain,
    ln2_bias,
    w_fc,
    fc_bias,
    w_proj,
    proj_bias,
    cotangent,
):
    row_place = lax.axis_index("row")
    col_place = lax.axis_index("col")
    row_devices = lax.axis_size("row")
    col_devices = lax.axis_size("col")
    width_row, local_rows = tokens.shape
    width_col = w_qkv.shape[2]
    hidden_col = w_fc.shape[1]
    seq_rows = local_rows * col_devices // row_devices
    seq_count = seq_rows // LEN
    residual = tokens.T.astype(jnp.float32)
    cotangent_local = cotangent.T
    first_gain = take_portion(ln1_gain, row_place, width_row, 0)
    first_normed, first_unit, first_inverse = norm_forward(
        residual, first_gain, take_portion(ln1_bias, row_place, width_row, 0), feature_totals
    )
    first_gathered = column_rows(first_normed.astype(jnp.bfloat16))

    def qkv_term(first_row, row_count):
        return jnp.einsum("td,sde->tse", first_gathered, w_qkv, preferred_element_type=jnp.float32)

    bias_col = take_portion(qv_bias, col_place, width_col, 1)
    bias_rows = jnp.stack([bias_col[0], jnp.zeros_like(bias_col[0]), bias_col[1]])
    qkv_sum = summed_over_row(qkv_term, seq_rows)
    qkv = (qkv_sum + bias_rows).astype(jnp.bfloat16)
    blocks = qkv.reshape(seq_count, LEN, 3, width_col)
    attn_blocks, log_totals = lax.map(attend_forward, (blocks, prefix))
    attn = attn_blocks.reshape(seq_rows, width_col)
    attn_gathered = row_rows(attn)

    def out_term(first_row, row_count):
        return jnp.dot(attn_gathered, w_out, preferred_element_type=jnp.float32)

    middle = (
        residual
        + summed_over_col(out_term, local_rows)
        + take_portion(out_bias, row_place, width_row, 0)
    )
    grad_output = cotangent_local.astype(jnp.float32)
    second_gain = take_portion(ln2_gain, row_place, width_row, 0)
    second_normed, second_unit, second_inverse = norm_forward(
        middle, second_gain, take_portion(ln2_bias, row_place, width_row, 0), feature_totals
    )
    second_gathered = column_rows(second_normed.astype(jnp.bfloat16))

    def up_term(first_row, row_count):
        return jnp.dot(second_gathered, w_fc, preferred_element_type=jnp.float32)

    hidden = summed_over_row(up_term, seq_rows) + take_portion(fc_bias, col_place, hidden_col, 0)
    active, gelu_pull = jax.vjp(gelu_tanh, hidden)
    active_gathered = row_rows(active.astype(jnp.bfloat16))

    def down_term(first_row, row_count):
        return jnp.einsum("tf,df->td", active_gathered, w_proj, preferred_element_type=jnp.float32)

    final_rows = (
        middle
        + summed_over_col(down_term, local_rows)
        + take_portion(proj_bias, row_place, width_row, 0)
    )
    output = final_rows.astype(jnp.bfloat16)
    grad_gathered = column_rows(cotangent_local)
    w_proj_grad = jnp.einsum(
        "tf,td->df", active_gathered, grad_gathered, preferred_element_type=jnp.float32
    )

    def active_term(first_row, row_count):
        return jnp.einsum("td,df->tf", grad_gathered, w_proj, preferred_element_type=jnp.float32)

    hidden_grad = gelu_pull(summed_over_row(active_term, seq_rows))[0].astype(jnp.bfloat16)
    hidden_gathered = row_rows(hidden_grad)
    w_fc_grad = jnp.einsum(
        "td,tf->df", second_gathered, hidden_gathered, preferred_element_type=jnp.float32
    )

    def second_term(first_row, row_count):
        return jnp.einsum("tf,df->td", hidden_gathered, w_fc, preferred_element_type=jnp.float32)

    second_grad = summed_over_col(second_term, local_rows)
    middle_grad = grad_output + norm_backward(
        second_grad, second_unit, second_inverse, second_gain, feature_totals
    )
    ln2_gain_part = place_portion(jnp.sum(second_grad * second_unit, axis=0), row_place, D, 0)
    ln2_bias_part = place_portion(jnp.sum(second_grad, axis=0), row_place, D, 0)
    fc_bias_part = place_portion(jnp.sum(hidden_grad.astype(jnp.float32), axis=0), col_place, FF, 0)
    proj_bias_part = place_portion(jnp.sum(grad_output, axis=0), row_place, D, 0)
    branch_grad = middle_grad.astype(jnp.bfloat16)
    branch_gathered = column_rows(branch_grad)
    w_out_grad = jnp.einsum(
        "te,td->ed", attn_gathered, branch_gathered, preferred_element_type=jnp.float32
    )

    def attn_term(first_row, row_count):
        return jnp.einsum("td,ed->te", branch_gathered, w_out, preferred_element_type=jnp.float32)

    attn_grad = summed_over_row(attn_term, seq_rows).astype(jnp.bfloat16)
    qkv_grad = lax.map(
        attend_backward, (blocks, prefix, log_totals, attn_grad.reshape(seq_count, LEN, width_col))
    )
    qkv_grad = qkv_grad.reshape(seq_rows, 3, width_col)
    qkv_gathered = row_rows(qkv_grad)
    w_qkv_grad = jnp.einsum(
        "td,tse->sde", first_gathered, qkv_gathered, preferred_element_type=jnp.float32
    )

    def first_term(first_row, row_count):
        return jnp.einsum("tse,sde->td", qkv_gathered, w_qkv, preferred_element_type=jnp.float32)

    first_grad = summed_over_col(first_term, local_rows)
    input_grad = middle_grad + norm_backward(
        first_grad, first_unit, first_inverse, first_gain, feature_totals
    )
    qkv_totals = jnp.sum(qkv_grad.astype(jnp.float32), axis=0)
    qv_part = place_portion(jnp.stack([qkv_totals[0], qkv_totals[2]]), col_place, D, 1)
    out_bias_part = place_portion(jnp.sum(branch_grad.astype(jnp.float32), axis=0), row_place, D, 0)
    ln1_gain_part = place_portion(jnp.sum(first_grad * first_unit, axis=0), row_place, D, 0)
    ln1_bias_part = place_portion(jnp.sum(first_grad, axis=0), row_place, D, 0)
    vectors = lax.psum(
        (
            ln1_gain_part,
            ln1_bias_part,
            qv_part,
            out_bias_part,
            ln2_gain_part,
            ln2_bias_part,
            fc_bias_part,
            proj_bias_part,
        ),
        ("dp", "row", "col"),
    )
    matrices = (
        lax.psum(w_qkv_grad.astype(jnp.bfloat16), "dp").astype(jnp.float32),
        lax.psum(w_out_grad.astype(jnp.bfloat16), "dp").astype(jnp.float32),
        lax.psum(w_fc_grad.astype(jnp.bfloat16), "dp").astype(jnp.float32),
        lax.psum(w_proj_grad.astype(jnp.bfloat16), "dp").astype(jnp.float32),
    )
    return (
        output.T,
        input_grad.T,
        vectors[0],
        vectors[1],
        matrices[0],
        vectors[2],
        matrices[1],
        vectors[3],
        vectors[4],
        vectors[5],
        matrices[2],
        vectors[6],
        matrices[3],
        vectors[7],
    )


def solution(mesh):
    placed = (
        P("row", ("dp", "col")),
        P(("dp", "row")),
        P(),
        P(),
        P(None, "row", "col"),
        P(),
        P("col", "row"),
        P(),
        P(),
        P(),
        P("row", "col"),
        P(),
        P("row", "col"),
        P(),
        P("row", ("dp", "col")),
    )
    return jax.shard_map(
        on_device,
        mesh=mesh,
        in_specs=placed,
        out_specs=(
            P("row", ("dp", "col")),
            P("row", ("dp", "col")),
            P(),
            P(),
            P(None, "row", "col"),
            P(),
            P("col", "row"),
            P(),
            P(),
            P(),
            P("row", "col"),
            P(),
            P("row", "col"),
            P(),
        ),
        check_vma=False,
    )
```

profile of v0, /device:TPU:0, one launch (start us, length us, event | category | flops | bytes accessed | tf_op | source)
XLA Modules:
  0.0 1165.3 jit_solution(17599242956197801233)
XLA Ops:
  11.0 11.5 all-reduce.4
  22.5 1.9 fusion.38
  25.6 35.4 %all-gather.9.cloned.1.call-done = bf16[4096,192]{0,1:T(8,128)(2,1)} async-done(((bf16[1024,192]{0,1:T(8,128)(2,1)}), bf16[4096,192]{0,1:T(8,128)(2,1)}) %all-gather.9.cloned.1.call-update) | async-done | bytes 1572880 | tf_op jit(solution)/shard_map/all_gather | solution.py:19
  61.1 6.4 fusion.61
  69.5 92.0 %reduce-scatter.9.cloned.1.call-done = f32[1024,3,192]{0,2,1:T(8,128)} async-done(((f32[4096,3,192]{0,2,1:T(8,128)}), f32[1024,3,192]{0,2,1:T(8,128)}) %reduce-scatter.9.cloned.1.call-update) | async-done | bytes 2359312 | tf_op jit(solution)/shard_map/reduce_scatter | solution.py:27
  161.5 1.9 add_convert_fusion
  163.5 3.2 fusion.55
  168.5 2.8 copy-done.2
  171.3 3.0 fusion.21
  174.4 31.1 %all-gather.11.cloned.1.call-done = bf16[4096,192]{0,1:T(8,128)(2,1)} async-done(((bf16[1024,192]{0,1:T(8,128)(2,1)}), bf16[4096,192]{0,1:T(8,128)(2,1)}) %all-gather.11.cloned.1.call-update) | async-done | bytes 1572880 | tf_op jit(solution)/shard_map/all_gather | solution.py:23
  205.5 3.7 fusion.56
  212.1 57.5 %reduce-scatter.11.cloned.1.call-done = f32[1024,192]{0,1:T(8,128)} async-done(((f32[4096,192]{0,1:T(8,128)}), f32[1024,192]{0,1:T(8,128)}) %reduce-scatter.11.cloned.1.call-update) | async-done | bytes 786448 | tf_op jit(solution)/shard_map/reduce_scatter | solution.py:36
  270.9 10.1 all-reduce.3
  282.1 26.1 %all-gather.17.cloned.1.call-done = bf16[4096,192]{0,1:T(8,128)(2,1)} async-done(((bf16[1024,192]{0,1:T(8,128)(2,1)}), bf16[4096,192]{0,1:T(8,128)(2,1)}) %all-gather.17.cloned.1.call-update) | async-done | bytes 1572880 | tf_op jit(solution)/shard_map/all_gather | solution.py:19
  308.2 7.7 fusion.59
  316.2 30.0 %all-gather.13.cloned.1.call-done = bf16[4096,192]{0,1:T(8,128)(2,1)} async-done(((bf16[1024,192]{0,1:T(8,128)(2,1)}), bf16[4096,192]{0,1:T(8,128)(2,1)}) %all-gather.13.cloned.1.call-update) | async-done | bytes 1572880 | tf_op jit(solution)/shard_map/all_gather | solution.py:19
  346.2 7.9 fusion.57
  354.9 114.0 %reduce-scatter.17.cloned.1.call-done = f32[1024,768]{1,0:T(8,128)} async-done(((f32[4096,768]{1,0:T(8,128)}), f32[1024,768]{1,0:T(8,128)}) %reduce-scatter.17.cloned.1.call-update) | async-done | bytes 3145744 | tf_op jit(solution)/shard_map/reduce_scatter | solution.py:27
  468.9 123.9 %reduce-scatter.13.cloned.1.call-done = f32[1024,768]{1,0:T(8,128)} async-done(((f32[4096,768]{1,0:T(8,128)}), f32[1024,768]{1,0:T(8,128)}) %reduce-scatter.13.cloned.1.call-update) | async-done | bytes 3145744 | tf_op jit(solution)/shard_map/reduce_scatter | solution.py:27
  592.7 5.6 convert_reduce_fusion
  598.5 70.2 %all-gather.19.cloned.1.call-done = bf16[4096,768]{1,0:T(8,128)(2,1)} async-done(((bf16[1024,768]{1,0:T(8,128)(2,1)}), bf16[4096,768]{1,0:T(8,128)(2,1)}) %all-gather.19.cloned.1.call-update) | async-done | bytes 6291472 | tf_op jit(solution)/shard_map/all_gather | solution.py:23
  668.7 6.6 fusion.60
  675.4 60.4 %reduce-scatter.19.cloned.1.call-done = f32[1024,192]{0,1:T(8,128)} async-done(((f32[4096,192]{0,1:T(8,128)}), f32[1024,192]{0,1:T(8,128)}) %reduce-scatter.19.cloned.1.call-update) | async-done | bytes 786448 | tf_op jit(solution)/shard_map/reduce_scatter | solution.py:36
  737.3 10.1 all-reduce.2
  747.3 2.2 convert_reduce_fusion.4
  749.7 35.4 %all-gather.21.cloned.1.call-done = bf16[4096,192]{0,1:T(8,128)(2,1)} async-done(((bf16[1024,192]{0,1:T(8,128)(2,1)}), bf16[4096,192]{0,1:T(8,128)(2,1)}) %all-gather.21.cloned.1.call-update) | async-done | bytes 1572880 | tf_op jit(solution)/shard_map/all_gather | solution.py:19
  785.0 3.7 fusion.62
  789.8 41.9 %reduce-scatter.21.cloned.1.call-done = f32[1024,192]{0,1:T(8,128)} async-done(((f32[4096,192]{0,1:T(8,128)}), f32[1024,192]{0,1:T(8,128)}) %reduce-scatter.21.cloned.1.call-update) | async-done | bytes 786448 | tf_op jit(solution)/shard_map/reduce_scatter | solution.py:27
  833.0 6.1 multiply_reduce_fusion
  841.8 5.2 multiply_convert_fusion
  847.0 4.2 fusion.16
  851.6 2.0 fusion.17
  853.7 2.1 fusion.18
  857.6 4.9 convolution_convert_fusion.1
  862.4 41.3 %all-gather.15.cloned.1.call-done = bf16[4096,768]{1,0:T(8,128)(2,1)} async-done(((bf16[1024,768]{1,0:T(8,128)(2,1)}), bf16[4096,768]{1,0:T(8,128)(2,1)}) %all-gather.15.cloned.1.call-update) | async-done | bytes 6291472 | tf_op jit(solution)/shard_map/all_gather | solution.py:23
  903.8 5.5 fusion.25
  910.5 52.1 %all-gather.23.cloned.1.call-done = bf16[4096,3,192]{0,2,1:T(8,128)(2,1)} async-done(((bf16[1024,3,192]{0,2,1:T(8,128)(2,1)}), bf16[4096,3,192]{0,2,1:T(8,128)(2,1)}) %all-gather.23.cloned.1.call-update) | async-done | bytes 4718608 | tf_op jit(solution)/shard_map/all_gather | solution.py:23
  962.6 5.0 fusion.26
  967.9 5.4 convolution_bitcast_fusion
  974.3 6.8 fusion.58
  983.0 4.3 all-reduce.8.cloned.1.call-done
  987.3 1.8 convert_element_type.122
  990.9 1.9 copy.34
  994.5 56.6 %reduce-scatter.23.cloned.1.call-done = f32[1024,192]{0,1:T(8,128)} async-done(((f32[4096,192]{0,1:T(8,128)}), f32[1024,192]{0,1:T(8,128)}) %reduce-scatter.23.cloned.1.call-update) | async-done | bytes 786448 | tf_op jit(solution)/shard_map/reduce_scatter | solution.py:36
  1052.5 10.1 all-reduce.1
  1062.7 51.0 %reduce-scatter.15.cloned.1.call-done = f32[1024,192]{0,1:T(8,128)} async-done(((f32[4096,192]{0,1:T(8,128)}), f32[1024,192]{0,1:T(8,128)}) %reduce-scatter.15.cloned.1.call-update) | async-done | bytes 786448 | tf_op jit(solution)/shard_map/reduce_scatter | solution.py:36
  1113.6 2.9 fusion.43
  1117.1 41.7 %all-reduce = (f32[768]{0:T(1024)}, f32[768]{0:T(1024)}, f32[2,768]{1,0:T(2,128)}, f32[768]{0:T(1024)}, f32[768]{0:T(1024)}, /*index=5*/f32[768]{0:T(1024)}, f32[3072]{0:T(1024)}, f32[768]{0:T(1024)}) all-reduce(f32[768]{0:T(1024)S(1)} %dynamic_update_slice.33, ...), channel_id=1, replica_groups=mesh['dp'=2,'row'=4,'col'=4] {'dp','row','col'}, use_global_device_ids=true, to_apply=%region_28.29 | all-reduce | flops 9216 | bytes 73728 | tf_op jit(solution)/shard_map/psum | solution.py:264
  (126 shorter events, 33.4 us)
Async XLA Ops:
  7.2 339.0 %copy-start = (bf16[192,768]{1,0:T(8,128)(2,1)S(1)}, bf16[192,768]{1,0:T(8,128)(2,1)}, u32[]{:S(2)}) copy-start(bf16[192,768]{1,0:T(8,128)(2,1)} %param.25) | copy-start | bytes 884740
  7.2 53.9 %all-gather.9.cloned.1.call-start = ((), (), s32[]{:S(2)}) async-start(), calls=%async_computation.8 | async-start | bytes 1966080 | tf_op jit(solution)/shard_map/all_gather | solution.py:19
  24.4 137.1 %reduce-scatter.9.cloned.1.call-start = ((), (), s32[]{:S(2)}) async-start(), calls=%async_computation.9 | async-start | bytes 11796480 | tf_op jit(solution)/shard_map/reduce_scatter | solution.py:27
  67.5 137.9 %all-gather.11.cloned.1.call-start = ((), (), s32[]{:S(2)}) async-start(), calls=%async_computation.10 | async-start | bytes 1966080 | tf_op jit(solution)/shard_map/all_gather | solution.py:23
  163.5 3.3 copy-start.8
  163.5 5.0 copy-start.11
  166.7 4.6 copy-start.2
  171.3 34.1 %copy-start.17 = (bf16[192,192]{1,0:T(8,128)(2,1)S(1)}, bf16[192,192]{1,0:T(8,128)(2,1)}, u32[]{:S(2)}) copy-start(bf16[192,192]{1,0:T(8,128)(2,1)} %param.21) | copy-start | bytes 221188
  174.3 95.3 %reduce-scatter.11.cloned.1.call-start = ((), (), s32[]{:S(2)}) async-start(), calls=%async_computation.11 | async-start | bytes 3932160 | tf_op jit(solution)/shard_map/reduce_scatter | solution.py:36
  209.2 60.4 %copy-start.4 = (bf16[192,1024]{1,0:T(8,128)(2,1)S(1)}, bf16[192,1024]{1,0:T(8,128)(2,1)}, u32[]{:S(2)}) copy-start(bf16[192,1024]{1,0:T(8,128)(2,1)} %param.15) | copy-start | bytes 1179652
  209.2 99.0 %copy-start.15 = (bf16[192,768]{1,0:T(8,128)(2,1)S(1)}, bf16[192,768]{1,0:T(8,128)(2,1)}, u32[]{:S(2)}) copy-start(bf16[192,768]{1,0:T(8,128)(2,1)} %param.27) | copy-start | bytes 884740
  209.2 99.0 %all-gather.17.cloned.1.call-start = ((), (), s32[]{:S(2)}) async-start(), calls=%async_computation.16 | async-start | bytes 1966080 | tf_op jit(solution)/shard_map/all_gather | solution.py:19
  209.8 136.4 %all-gather.13.cloned.1.call-start = ((), (), s32[]{:S(2)}) async-start(), calls=%async_computation.12 | async-start | bytes 1966080 | tf_op jit(solution)/shard_map/all_gather | solution.py:19
  282.0 186.9 %reduce-scatter.17.cloned.1.call-start = ((), (), s32[]{:S(2)}) async-start(), calls=%async_computation.17 | async-start | bytes 15728640 | tf_op jit(solution)/shard_map/reduce_scatter | solution.py:27
  315.9 276.8 %reduce-scatter.13.cloned.1.call-start = ((), (), s32[]{:S(2)}) async-start(), calls=%async_computation.13 | async-start | bytes 15728640 | tf_op jit(solution)/shard_map/reduce_scatter | solution.py:27
  354.0 314.7 %all-gather.19.cloned.1.call-start = ((), (), s32[]{:S(2)}) async-start(), calls=%async_computation.18 | async-start | bytes 7864320 | tf_op jit(solution)/shard_map/all_gather | solution.py:23
  598.4 137.4 %reduce-scatter.19.cloned.1.call-start = ((), (), s32[]{:S(2)}) async-start(), calls=%async_computation.19 | async-start | bytes 3932160 | tf_op jit(solution)/shard_map/reduce_scatter | solution.py:36
  675.3 72.0 %copy-start.7 = (bf16[192,1024]{1,0:T(8,128)(2,1)S(1)}, bf16[192,1024]{1,0:T(8,128)(2,1)}, u32[]{:S(2)}) copy-start(bf16[192,1024]{1,0:T(8,128)(2,1)} %param.29) | copy-start | bytes 1179652
  675.4 109.6 %all-gather.21.cloned.1.call-start = ((), (), s32[]{:S(2)}) async-start(), calls=%async_computation.20 | async-start | bytes 1966080 | tf_op jit(solution)/shard_map/all_gather | solution.py:19
  749.6 82.1 %reduce-scatter.21.cloned.1.call-start = ((), (), s32[]{:S(2)}) async-start(), calls=%async_computation.21 | async-start | bytes 3932160 | tf_op jit(solution)/shard_map/reduce_scatter | solution.py:27
  788.7 44.2 %copy-start.12 = (bf16[1024,1,192]{0,2,1:T(8,128)(2,1)S(1)}, bf16[1024,1,192]{0,2,1:T(8,128)(2,1)}, u32[]{:S(2)}) copy-start(bf16[1024,1,192]{0,2,1:T(8,128)(2,1)} %copy-done.11) | copy-start | bytes 1179652
  788.8 115.0 %all-gather.15.cloned.1.call-start = ((), (), s32[]{:S(2)}) async-start(), calls=%async_computation.14 | async-start | bytes 7864320 | tf_op jit(solution)/shard_map/all_gather | solution.py:23
  789.5 173.0 %all-gather.23.cloned.1.call-start = ((), (), s32[]{:S(2)}) async-start(), calls=%async_computation.22 | async-start | bytes 5898240 | tf_op jit(solution)/shard_map/all_gather | solution.py:23
  832.9 6.2 slice-start
  832.9 7.1 slice-start.1
  833.0 8.8 slice-start.2
  841.8 5.2 copy-start.9
  847.0 4.6 copy-start.3
  855.7 1.8 copy-start.10
  857.0 130.3 %all-reduce.8.cloned.1.call-start = ((), (), s32[]{:S(2)}) async-start(), calls=%async_computation.24 | async-start | bytes 1966080 | tf_op jit(solution)/shard_map/psum | solution.py:278
  862.4 46.8 %copy-start.6 = (bf16[4096,192]{0,1:T(8,128)(2,1)S(1)}, bf16[4096,192]{0,1:T(8,128)(2,1)}, u32[]{:S(2)}) copy-start(bf16[4096,192]{0,1:T(8,128)(2,1)} %all-gather.11.cloned.1.call-done) | copy-start | bytes 4718596
  903.8 5.5 copy-start.13
  910.5 57.4 %copy-start.14 = (bf16[3,192,192]{2,1,0:T(8,128)(2,1)S(1)}, bf16[3,192,192]{2,1,0:T(8,128)(2,1)}, u32[]{:S(2)}) copy-start(bf16[3,192,192]{2,1,0:T(8,128)(2,1)} %param.19) | copy-start | bytes 663556
  967.5 83.5 %reduce-scatter.23.cloned.1.call-start = ((), (), s32[]{:S(2)}) async-start(), calls=%async_computation.23 | async-start | bytes 3932160 | tf_op jit(solution)/shard_map/reduce_scatter | solution.py:36
  973.3 1.0 copy-start.16
  973.3 140.3 %reduce-scatter.15.cloned.1.call-start = ((), (), s32[]{:S(2)}) async-start(), calls=%async_computation.15 | async-start | bytes 3932160 | tf_op jit(solution)/shard_map/reduce_scatter | solution.py:36
  981.1 132.5 %copy-start.5 = (f32[1024,192]{0,1:T(8,128)S(1)}, f32[1024,192]{0,1:T(8,128)}, u32[]{:S(2)}) copy-start(f32[1024,192]{0,1:T(8,128)} %reduce-scatter.19.cloned.1.call-done) | copy-start | bytes 2359300
  992.8 165.9 %copy-start.1 = (bf16[192,768]{1,0:T(8,128)(2,1)S(1)}, bf16[192,768]{1,0:T(8,128)(2,1)}, u32[]{:S(2)}) copy-start(bf16[192,768]{1,0:T(8,128)(2,1)} %param.25) | copy-start | bytes 884740
Sparse Core Ops, SparseCore 0:
  24.6 36.4 all-gather.8
  67.6 93.8 reduce-scatter.8
  174.4 30.9 all-gather.10
  209.3 60.2 reduce-scatter.10
  271.0 37.1 all-gather.16
  310.2 35.9 all-gather.12
  349.3 119.5 reduce-scatter.16
  472.0 120.7 reduce-scatter.12
  598.5 70.1 all-gather.18
  675.5 60.2 reduce-scatter.18
  749.7 35.2 all-gather.20
  788.9 42.8 reduce-scatter.20
  833.6 70.1 all-gather.14
  905.5 57.0 all-gather.22
  967.7 19.5 all-reduce.7
  989.5 61.4 reduce-scatter.22
  1053.3 60.2 reduce-scatter.14
where the time goes:
time: 1170 us
  waiting for transfers between devices  924 us (79%)
  matrix products  85.4 us (7%)
  blocking collectives  83.4 us (7%)
  other arithmetic  37.2 us (3%)
  local copies, waits for them, and re-layouts  18.6 us (2%)
  between operations  15 us (1%)
    reduce_scatter x4, waiting for transfers between devices, summed_over_row(): lax.psum_scatter(term_fn(jnp.int32(0), row_count * lax.axis_size('row')),...  372 us
    reduce_scatter x4, waiting for transfers between devices, summed_over_col(): lax.psum_scatter(term_fn(jnp.int32(0), row_count * lax.axis_size('col')),...  225 us
    all_gather x4, waiting for transfers between devices, row_rows(): return lax.all_gather(values, 'row', axis=0, tiled=True)  195 us
    all_gather x4, waiting for transfers between devices, column_rows(): return lax.all_gather(values, 'col', axis=0, tiled=True)  127 us
    psum x4, blocking collectives, feature_totals(): return lax.psum(values, 'row')  41.7 us
    psum x1, blocking collectives, on_device(): lax.psum((ln1_gain_part, ln1_bias_part, qv_part, out_bias_part, ln2_gain_...  41.7 us
  transfers between devices with their start and end apart: 17, of which 17 were waited for; matrix products, arithmetic and copies ran while one was open for 7% of the time, Pallas kernels for 0%

commit v1 on v0

--- a/solution.py
+++ b/solution.py
@@ -261,7 +261,13 @@
     out_bias_part = place_portion(jnp.sum(branch_grad.astype(jnp.float32), axis=0), row_place, D, 0)
     ln1_gain_part = place_portion(jnp.sum(first_grad * first_unit, axis=0), row_place, D, 0)
     ln1_bias_part = place_portion(jnp.sum(first_grad, axis=0), row_place, D, 0)
-    vectors = lax.psum(
+
+    def spread_local_data(sheet):
+        for at in (("row", "col"), "dp"):
+            sheet = lax.psum(sheet, at)
+        return sheet
+
+    vectors = spread_local_data(
         (
             ln1_gain_part,
             ln1_bias_part,
@@ -271,8 +277,7 @@
             ln2_bias_part,
             fc_bias_part,
             proj_bias_part,
-        ),
-        ("dp", "row", "col"),
+        )
     )
     matrices = (
         lax.psum(w_qkv_grad.astype(jnp.bfloat16), "dp").astype(jnp.float32),

time: 1170 us -> 1210 us (1.034)
  blocking collectives: 83.4 us -> 122 us
    psum x1 -> x2, blocking collectives: 41.7 us -> 80.4 us  [spread_local_data(): sheet = lax.psum(sheet, at)]
where the time goes in v1:
time: 1210 us; the launch traced here: 1200 us
  waiting for transfers between devices  924 us (76%)
  blocking collectives  122 us (10%)
  matrix products  85.4 us (7%)
  other arithmetic  37.2 us (3%)
  local copies, waits for them, and re-layouts  18.6 us (2%)
  between operations  15 us (1%)
    reduce_scatter x4, waiting for transfers between devices, summed_over_row(): lax.psum_scatter(term_fn(jnp.int32(0), row_count * lax.axis_size('row')),...  372 us
    reduce_scatter x4, waiting for transfers between devices, summed_over_col(): lax.psum_scatter(term_fn(jnp.int32(0), row_count * lax.axis_size('col')),...  225 us
    all_gather x4, waiting for transfers between devices, row_rows(): return lax.all_gather(values, 'row', axis=0, tiled=True)  195 us
    all_gather x4, waiting for transfers between devices, column_rows(): return lax.all_gather(values, 'col', axis=0, tiled=True)  127 us
    psum x2, blocking collectives, spread_local_data(): sheet = lax.psum(sheet, at)  80.4 us
    psum x4, blocking collectives, feature_totals(): return lax.psum(values, 'row')  41.7 us
  transfers between devices with their start and end apart: 17, of which 17 were waited for; matrix products, arithmetic and copies ran while one was open for 7% of the time, Pallas kernels for 0%

profile of v1, /device:TPU:0, one launch (start us, length us, event | category | flops | bytes accessed | tf_op | source)
XLA Modules:
  0.0 1204.0 jit_solution(6226446289495670372)
XLA Ops:
  11.0 11.5 all-reduce.4
  22.5 1.9 fusion.38
  25.6 35.4 %all-gather.9.cloned.1.call-done = bf16[4096,192]{0,1:T(8,128)(2,1)} async-done(((bf16[1024,192]{0,1:T(8,128)(2,1)}), bf16[4096,192]{0,1:T(8,128)(2,1)}) %all-gather.9.cloned.1.call-update) | async-done | bytes 1572880 | tf_op jit(solution)/shard_map/all_gather | solution.py:19
  61.1 6.4 fusion.61
  69.5 92.0 %reduce-scatter.9.cloned.1.call-done = f32[1024,3,192]{0,2,1:T(8,128)} async-done(((f32[4096,3,192]{0,2,1:T(8,128)}), f32[1024,3,192]{0,2,1:T(8,128)}) %reduce-scatter.9.cloned.1.call-update) | async-done | bytes 2359312 | tf_op jit(solution)/shard_map/reduce_scatter | solution.py:27
  161.5 1.9 add_convert_fusion
  163.5 3.2 fusion.55
  168.5 2.8 copy-done.2
  171.3 3.0 fusion.21
  174.4 31.1 %all-gather.11.cloned.1.call-done = bf16[4096,192]{0,1:T(8,128)(2,1)} async-done(((bf16[1024,192]{0,1:T(8,128)(2,1)}), bf16[4096,192]{0,1:T(8,128)(2,1)}) %all-gather.11.cloned.1.call-update) | async-done | bytes 1572880 | tf_op jit(solution)/shard_map/all_gather | solution.py:23
  205.5 3.7 fusion.56
  212.1 57.5 %reduce-scatter.11.cloned.1.call-done = f32[1024,192]{0,1:T(8,128)} async-done(((f32[4096,192]{0,1:T(8,128)}), f32[1024,192]{0,1:T(8,128)}) %reduce-scatter.11.cloned.1.call-update) | async-done | bytes 786448 | tf_op jit(solution)/shard_map/reduce_scatter | solution.py:36
  270.9 10.1 all-reduce.3
  282.1 26.1 %all-gather.17.cloned.1.call-done = bf16[4096,192]{0,1:T(8,128)(2,1)} async-done(((bf16[1024,192]{0,1:T(8,128)(2,1)}), bf16[4096,192]{0,1:T(8,128)(2,1)}) %all-gather.17.cloned.1.call-update) | async-done | bytes 1572880 | tf_op jit(solution)/shard_map/all_gather | solution.py:19
  308.2 7.7 fusion.59
  316.2 30.0 %all-gather.13.cloned.1.call-done = bf16[4096,192]{0,1:T(8,128)(2,1)} async-done(((bf16[1024,192]{0,1:T(8,128)(2,1)}), bf16[4096,192]{0,1:T(8,128)(2,1)}) %all-gather.13.cloned.1.call-update) | async-done | bytes 1572880 | tf_op jit(solution)/shard_map/all_gather | solution.py:19
  346.2 7.9 fusion.57
  354.9 114.0 %reduce-scatter.17.cloned.1.call-done = f32[1024,768]{1,0:T(8,128)} async-done(((f32[4096,768]{1,0:T(8,128)}), f32[1024,768]{1,0:T(8,128)}) %reduce-scatter.17.cloned.1.call-update) | async-done | bytes 3145744 | tf_op jit(solution)/shard_map/reduce_scatter | solution.py:27
  468.9 123.9 %reduce-scatter.13.cloned.1.call-done = f32[1024,768]{1,0:T(8,128)} async-done(((f32[4096,768]{1,0:T(8,128)}), f32[1024,768]{1,0:T(8,128)}) %reduce-scatter.13.cloned.1.call-update) | async-done | bytes 3145744 | tf_op jit(solution)/shard_map/reduce_scatter | solution.py:27
  592.7 5.6 convert_reduce_fusion
  598.5 70.2 %all-gather.19.cloned.1.call-done = bf16[4096,768]{1,0:T(8,128)(2,1)} async-done(((bf16[1024,768]{1,0:T(8,128)(2,1)}), bf16[4096,768]{1,0:T(8,128)(2,1)}) %all-gather.19.cloned.1.call-update) | async-done | bytes 6291472 | tf_op jit(solution)/shard_map/all_gather | solution.py:23
  668.7 6.6 fusion.60
  675.4 60.4 %reduce-scatter.19.cloned.1.call-done = f32[1024,192]{0,1:T(8,128)} async-done(((f32[4096,192]{0,1:T(8,128)}), f32[1024,192]{0,1:T(8,128)}) %reduce-scatter.19.cloned.1.call-update) | async-done | bytes 786448 | tf_op jit(solution)/shard_map/reduce_scatter | solution.py:36
  737.3 10.1 all-reduce.2
  747.3 2.2 convert_reduce_fusion.4
  749.7 35.4 %all-gather.21.cloned.1.call-done = bf16[4096,192]{0,1:T(8,128)(2,1)} async-done(((bf16[1024,192]{0,1:T(8,128)(2,1)}), bf16[4096,192]{0,1:T(8,128)(2,1)}) %all-gather.21.cloned.1.call-update) | async-done | bytes 1572880 | tf_op jit(solution)/shard_map/all_gather | solution.py:19
  785.0 3.7 fusion.62
  789.8 41.9 %reduce-scatter.21.cloned.1.call-done = f32[1024,192]{0,1:T(8,128)} async-done(((f32[4096,192]{0,1:T(8,128)}), f32[1024,192]{0,1:T(8,128)}) %reduce-scatter.21.cloned.1.call-update) | async-done | bytes 786448 | tf_op jit(solution)/shard_map/reduce_scatter | solution.py:27
  833.0 6.1 multiply_reduce_fusion
  841.8 5.2 multiply_convert_fusion
  847.0 4.2 fusion.16
  851.6 2.0 fusion.17
  853.7 2.1 fusion.18
  857.6 4.9 convolution_convert_fusion.1
  862.4 41.3 %all-gather.15.cloned.1.call-done = bf16[4096,768]{1,0:T(8,128)(2,1)} async-done(((bf16[1024,768]{1,0:T(8,128)(2,1)}), bf16[4096,768]{1,0:T(8,128)(2,1)}) %all-gather.15.cloned.1.call-update) | async-done | bytes 6291472 | tf_op jit(solution)/shard_map/all_gather | solution.py:23
  903.8 5.5 fusion.25
  910.5 52.1 %all-gather.23.cloned.1.call-done = bf16[4096,3,192]{0,2,1:T(8,128)(2,1)} async-done(((bf16[1024,3,192]{0,2,1:T(8,128)(2,1)}), bf16[4096,3,192]{0,2,1:T(8,128)(2,1)}) %all-gather.23.cloned.1.call-update) | async-done | bytes 4718608 | tf_op jit(solution)/shard_map/all_gather | solution.py:23
  962.6 5.0 fusion.26
  967.9 5.4 convolution_bitcast_fusion
  974.3 6.8 fusion.58
  983.0 4.3 all-reduce.9.cloned.1.call-done
  990.9 1.9 copy.34
  994.5 56.6 %reduce-scatter.23.cloned.1.call-done = f32[1024,192]{0,1:T(8,128)} async-done(((f32[4096,192]{0,1:T(8,128)}), f32[1024,192]{0,1:T(8,128)}) %reduce-scatter.23.cloned.1.call-update) | async-done | bytes 786448 | tf_op jit(solution)/shard_map/reduce_scatter | solution.py:36
  1052.5 10.1 all-reduce.1
  1062.7 51.0 %reduce-scatter.15.cloned.1.call-done = f32[1024,192]{0,1:T(8,128)} async-done(((f32[4096,192]{0,1:T(8,128)}), f32[1024,192]{0,1:T(8,128)}) %reduce-scatter.15.cloned.1.call-update) | async-done | bytes 786448 | tf_op jit(solution)/shard_map/reduce_scatter | solution.py:36
  1113.6 2.9 fusion.43
  1117.1 76.3 %all-reduce = (f32[768]{0:T(1024)S(1)}, f32[768]{0:T(1024)S(1)}, f32[2,768]{1,0:T(2,128)S(1)}, f32[768]{0:T(1024)S(1)}, f32[768]{0:T(1024)S(1)}, /*index=5*/f32[...) all-reduce(f32[768]{0:T(1024)S(1)} %dynamic_update_slice.33, ...), channel_id=1, replica_groups=mesh['dp'=2,'row'=4,'col'=4] {'row','col'}, use_global_device_ids=true, to_apply=%region_28.29 | all-reduce | flops 9216 | bytes 73728 | tf_op jit(solution)/shard_map/psum | solution.py:267
  1193.4 4.1 all-reduce.5
  (127 shorter events, 35.2 us)
Async XLA Ops:
  7.2 339.0 %copy-start = (bf16[192,768]{1,0:T(8,128)(2,1)S(1)}, bf16[192,768]{1,0:T(8,128)(2,1)}, u32[]{:S(2)}) copy-start(bf16[192,768]{1,0:T(8,128)(2,1)} %param.25) | copy-start | bytes 884740
  7.2 53.9 %all-gather.9.cloned.1.call-start = ((), (), s32[]{:S(2)}) async-start(), calls=%async_computation.8 | async-start | bytes 1966080 | tf_op jit(solution)/shard_map/all_gather | solution.py:19
  24.4 137.1 %reduce-scatter.9.cloned.1.call-start = ((), (), s32[]{:S(2)}) async-start(), calls=%async_computation.9 | async-start | bytes 11796480 | tf_op jit(solution)/shard_map/reduce_scatter | solution.py:27
  67.5 137.9 %all-gather.11.cloned.1.call-start = ((), (), s32[]{:S(2)}) async-start(), calls=%async_computation.10 | async-start | bytes 1966080 | tf_op jit(solution)/shard_map/all_gather | solution.py:23
  163.5 3.3 copy-start.8
  163.5 5.0 copy-start.11
  166.7 4.6 copy-start.2
  171.3 34.1 %copy-start.17 = (bf16[192,192]{1,0:T(8,128)(2,1)S(1)}, bf16[192,192]{1,0:T(8,128)(2,1)}, u32[]{:S(2)}) copy-start(bf16[192,192]{1,0:T(8,128)(2,1)} %param.21) | copy-start | bytes 221188
  174.3 95.3 %reduce-scatter.11.cloned.1.call-start = ((), (), s32[]{:S(2)}) async-start(), calls=%async_computation.11 | async-start | bytes 3932160 | tf_op jit(solution)/shard_map/reduce_scatter | solution.py:36
  209.2 60.4 %copy-start.4 = (bf16[192,1024]{1,0:T(8,128)(2,1)S(1)}, bf16[192,1024]{1,0:T(8,128)(2,1)}, u32[]{:S(2)}) copy-start(bf16[192,1024]{1,0:T(8,128)(2,1)} %param.15) | copy-start | bytes 1179652
  209.2 99.0 %copy-start.15 = (bf16[192,768]{1,0:T(8,128)(2,1)S(1)}, bf16[192,768]{1,0:T(8,128)(2,1)}, u32[]{:S(2)}) copy-start(bf16[192,768]{1,0:T(8,128)(2,1)} %param.27) | copy-start | bytes 884740
  209.2 99.0 %all-gather.17.cloned.1.call-start = ((), (), s32[]{:S(2)}) async-start(), calls=%async_computation.16 | async-start | bytes 1966080 | tf_op jit(solution)/shard_map/all_gather | solution.py:19
  209.8 136.4 %all-gather.13.cloned.1.call-start = ((), (), s32[]{:S(2)}) async-start(), calls=%async_computation.12 | async-start | bytes 1966080 | tf_op jit(solution)/shard_map/all_gather | solution.py:19
  282.0 186.9 %reduce-scatter.17.cloned.1.call-start = ((), (), s32[]{:S(2)}) async-start(), calls=%async_computation.17 | async-start | bytes 15728640 | tf_op jit(solution)/shard_map/reduce_scatter | solution.py:27
  315.9 276.8 %reduce-scatter.13.cloned.1.call-start = ((), (), s32[]{:S(2)}) async-start(), calls=%async_computation.13 | async-start | bytes 15728640 | tf_op jit(solution)/shard_map/reduce_scatter | solution.py:27
  354.0 314.7 %all-gather.19.cloned.1.call-start = ((), (), s32[]{:S(2)}) async-start(), calls=%async_computation.18 | async-start | bytes 7864320 | tf_op jit(solution)/shard_map/all_gather | solution.py:23
  598.4 137.4 %reduce-scatter.19.cloned.1.call-start = ((), (), s32[]{:S(2)}) async-start(), calls=%async_computation.19 | async-start | bytes 3932160 | tf_op jit(solution)/shard_map/reduce_scatter | solution.py:36
  675.3 72.0 %copy-start.7 = (bf16[192,1024]{1,0:T(8,128)(2,1)S(1)}, bf16[192,1024]{1,0:T(8,128)(2,1)}, u32[]{:S(2)}) copy-start(bf16[192,1024]{1,0:T(8,128)(2,1)} %param.29) | copy-start | bytes 1179652
  675.4 109.6 %all-gather.21.cloned.1.call-start = ((), (), s32[]{:S(2)}) async-start(), calls=%async_computation.20 | async-start | bytes 1966080 | tf_op jit(solution)/shard_map/all_gather | solution.py:19
  749.6 82.1 %reduce-scatter.21.cloned.1.call-start = ((), (), s32[]{:S(2)}) async-start(), calls=%async_computation.21 | async-start | bytes 3932160 | tf_op jit(solution)/shard_map/reduce_scatter | solution.py:27
  788.7 44.2 %copy-start.12 = (bf16[1024,1,192]{0,2,1:T(8,128)(2,1)S(1)}, bf16[1024,1,192]{0,2,1:T(8,128)(2,1)}, u32[]{:S(2)}) copy-start(bf16[1024,1,192]{0,2,1:T(8,128)(2,1)} %copy-done.11) | copy-start | bytes 1179652
  788.8 115.0 %all-gather.15.cloned.1.call-start = ((), (), s32[]{:S(2)}) async-start(), calls=%async_computation.14 | async-start | bytes 7864320 | tf_op jit(solution)/shard_map/all_gather | solution.py:23
  789.5 173.0 %all-gather.23.cloned.1.call-start = ((), (), s32[]{:S(2)}) async-start(), calls=%async_computation.22 | async-start | bytes 5898240 | tf_op jit(solution)/shard_map/all_gather | solution.py:23
  832.9 6.2 slice-start
  832.9 7.1 slice-start.1
  833.0 8.8 slice-start.2
  841.8 5.2 copy-start.9
  847.0 4.6 copy-start.3
  855.7 1.8 copy-start.10
  857.0 130.3 %all-reduce.9.cloned.1.call-start = ((), (), s32[]{:S(2)}) async-start(), calls=%async_computation.24 | async-start | bytes 1966080 | tf_op jit(solution)/shard_map/psum | solution.py:283
  862.4 46.8 %copy-start.6 = (bf16[4096,192]{0,1:T(8,128)(2,1)S(1)}, bf16[4096,192]{0,1:T(8,128)(2,1)}, u32[]{:S(2)}) copy-start(bf16[4096,192]{0,1:T(8,128)(2,1)} %all-gather.11.cloned.1.call-done) | copy-start | bytes 4718596
  903.8 5.5 copy-start.13
  910.5 57.4 %copy-start.14 = (bf16[3,192,192]{2,1,0:T(8,128)(2,1)S(1)}, bf16[3,192,192]{2,1,0:T(8,128)(2,1)}, u32[]{:S(2)}) copy-start(bf16[3,192,192]{2,1,0:T(8,128)(2,1)} %param.19) | copy-start | bytes 663556
  967.5 83.5 %reduce-scatter.23.cloned.1.call-start = ((), (), s32[]{:S(2)}) async-start(), calls=%async_computation.23 | async-start | bytes 3932160 | tf_op jit(solution)/shard_map/reduce_scatter | solution.py:36
  973.3 1.0 copy-start.16
  973.3 140.3 %reduce-scatter.15.cloned.1.call-start = ((), (), s32[]{:S(2)}) async-start(), calls=%async_computation.15 | async-start | bytes 3932160 | tf_op jit(solution)/shard_map/reduce_scatter | solution.py:36
  981.1 132.5 %copy-start.5 = (f32[1024,192]{0,1:T(8,128)S(1)}, f32[1024,192]{0,1:T(8,128)}, u32[]{:S(2)}) copy-start(f32[1024,192]{0,1:T(8,128)} %reduce-scatter.19.cloned.1.call-done) | copy-start | bytes 2359300
  992.8 204.6 %copy-start.1 = (bf16[192,768]{1,0:T(8,128)(2,1)S(1)}, bf16[192,768]{1,0:T(8,128)(2,1)}, u32[]{:S(2)}) copy-start(bf16[192,768]{1,0:T(8,128)(2,1)} %param.25) | copy-start | bytes 884740
Sparse Core Ops, SparseCore 0:
  24.6 36.4 all-gather.8
  67.6 93.8 reduce-scatter.8
  174.4 30.9 all-gather.10
  209.3 60.2 reduce-scatter.10
  271.0 37.1 all-gather.16
  310.2 35.9 all-gather.12
  349.3 119.5 reduce-scatter.16
  472.0 120.7 reduce-scatter.12
  598.5 70.1 all-gather.18
  675.5 60.2 reduce-scatter.18
  749.7 35.2 all-gather.20
  788.9 42.8 reduce-scatter.20
  833.6 70.1 all-gather.14
  905.5 57.0 all-gather.22
  967.7 19.5 all-reduce.8
  989.5 61.4 reduce-scatter.22
  1053.3 60.2 reduce-scatter.14
